TPU v7x, 256 devices: a whole 4x4x8 slice. The times are simulated.
256 devices in a mesh: sa: 2 (over y_lo), gx: 16 (over z, core), gy: 8 (over x, y_hi).
Axes of the slice: x: 4, y: 4 (y_hi: 2, y_lo: 2; y = y_hi * 2 + y_lo), z: 8, core: 2. Of those that a mesh axis runs over, the one named last changes fastest.
Arguments:
- pred_frames: float32 [12, 32768], P(None, ('sa', 'gx', 'gy')), parts along dimension 1, may hold values from -52 to 52, as said below
- true_frames: float32 [12, 32768], P(None, ('sa', 'gx', 'gy')), parts along dimension 1, may hold values from -52 to 52, as said below
- pred_atoms: float32 [3, 57344], P(None, ('sa', 'gx', 'gy')), parts along dimension 1, may hold values from -52 to 52
- true_atoms: float32 [3, 57344], P(None, ('sa', 'gx', 'gy')), parts along dimension 1, may hold values from -52 to 52
- atom_mask: int32 [57344], P(('sa', 'gx', 'gy')), parts along dimension 0, may hold values from 0 to 1, as said below
- residue_types: int32 [4096], P(('sa', 'gx', 'gy')), parts along dimension 0, may hold values from 0 to 19
- swap_flags: int32 [4096], P(('sa', 'gx', 'gy')), parts along dimension 0, may hold values from 0 to 1
Outputs:
- frame_loss: float32 [32768], P(('sa', 'gx', 'gy')), parts along dimension 0
- atom_loss: float32 [57344], P(('sa', 'gx', 'gy')), parts along dimension 0
- total_loss: float32 [2], P('sa'), parts along dimension 0
There are 2 independent parts, one for each index of `sa`. A program takes and returns all parts, laid end to end along the dimension named above; each array names one. Nothing has to cross between parts.
Inputs may be any that keep to these rules, and one draw needn't show every extreme that they name: `atom_mask`: atom slots 0 to 3 of every residue, its backbone atoms, are 1. `pred_frames`: rows 0 to 8 of each frame hold a rotation matrix, row-major; rows 9 to 11 its translation. `true_frames`: rows 0 to 8 of each frame hold a rotation matrix, row-major; rows 9 to 11 its translation.
All inputs are finite; a program needn't handle non-finite values.
Results may differ from a plain program's by a relative error of at most 0.0001.
Values sent between devices are 32-bit elements; how exact they have to be, the bound alone decides.
A program may use at most 64 MiB of HBM per device.

v0:
```python
import functools
import math
import jax
import jax.numpy as jnp
import numpy as np
from jax import lax
from jax.sharding import Mesh
from jax.sharding import PartitionSpec as P

GY = ("gy_0", "gy_1")
GX = ("gx_0", "gx_1")
GX_GY = ("gx_0", "gx_1", "gy_0", "gy_1")
SA_GX_GY = ("sa", "gx_0", "gx_1", "gy_0", "gy_1")
eps_square = 0.0001
clamp_length = 10.0


def side_by_side(arrays, axis, dim, along):
    widths = [a.shape[along] for a in arrays]
    both = jnp.concatenate(arrays, axis=along)
    result = lax.all_gather(both, axis, axis=dim, tiled=True)
    return tuple(jnp.split(result, [sum(widths[:k]) for k in range(1, len(widths))], axis=along))


def gather_turned(arrays, axis, dims):
    turned = [jnp.moveaxis(a, dim, 0) for a, dim in zip(arrays, dims)]
    both = jnp.concatenate([t.reshape(len(t), -1) for t in turned], axis=1)
    result, at, gathered = (lax.all_gather(both, axis, axis=0, tiled=True), 0, [])
    for t, dim in zip(turned, dims):
        piece = result[:, at : at + t[0].size].reshape(-1, *t.shape[1:])
        gathered.append(jnp.moveaxis(piece, 0, dim))
        at += t[0].size
    return tuple(gathered)


def split_up(value, dim, length):
    lengths = value.shape
    tiles = value.reshape(*lengths[:dim], length, lengths[dim] // length, *lengths[dim + 1 :])
    return jnp.moveaxis(tiles, dim, 0)


def sent_and_summed(value, axis, dim):
    tiles = split_up(value, dim, lax.axis_size(axis))
    arrived = lax.all_to_all(tiles, axis, split_axis=0, concat_axis=0, tiled=True)
    return arrived.sum(axis=0)


def by_axis(value, axes):
    return functools.reduce(lax.psum, axes, value)


def residue_tables():
    atom_counts = np.array([5, 11, 8, 8, 6, 9, 9, 4, 10, 8, 8, 9, 8, 11, 7, 6, 7, 14, 12, 7])
    chi_counts = np.array([0, 4, 2, 2, 1, 3, 3, 0, 2, 2, 2, 4, 3, 2, 2, 1, 1, 2, 2, 1])
    atom_table = (np.arange(14)[None, :] < atom_counts[:, None]).astype(np.float32)
    slot_ids = np.arange(8)[None, :]
    frame_table = (
        (slot_ids == 0) | (slot_ids == 3) | (slot_ids >= 4) & (slot_ids - 3 <= chi_counts[:, None])
    ).astype(np.float32)
    partner_table = np.tile(np.arange(14), (20, 1))
    for restype, swap_pairs in (
        (3, ((6, 7),)),
        (6, ((7, 8),)),
        (13, ((6, 7), (8, 9))),
        (18, ((6, 7), (8, 9))),
    ):
        for first_slot, second_slot in swap_pairs:
            partner_table[restype, first_slot] = second_slot
            partner_table[restype, second_slot] = first_slot
    flip_table = np.zeros((20, 8), np.float32)
    flip_table[3, 5] = 1.0
    flip_table[13, 5] = 1.0
    flip_table[18, 5] = 1.0
    flip_table[6, 6] = 1.0
    sign_table = np.array([1, -1, -1, 1, -1, -1, 1, -1, -1, 1, 1, 1], np.float32)
    return (atom_table, frame_table, partner_table, flip_table, sign_table)


def type_onehot(residue_types):
    return residue_types[:, None] == jnp.arange(20, dtype=jnp.int32)[None, :]


def frame_terms(pred_frames, true_frames, residue_types, swap_flags):
    tables = residue_tables()
    onehot = type_onehot(residue_types).astype(jnp.float32)
    frame_table = jnp.asarray(tables[1], dtype=jnp.float32)
    flip_table = jnp.asarray(tables[3], dtype=jnp.float32)
    sign_table = jnp.asarray(tables[4], dtype=jnp.float32)
    exists = jnp.sum(onehot[:, :, None] * frame_table[None], axis=1)
    flips = jnp.sum(onehot[:, :, None] * flip_table[None], axis=1) * swap_flags[:, None].astype(
        jnp.float32
    )
    residues = residue_types.shape[0]
    shaped = true_frames.reshape(12, residues, 8)
    resolved = jnp.where(flips[None] > 0.5, shaped * sign_table[:, None, None], shaped).reshape(
        12, residues * 8
    )
    rot_pred = pred_frames[:9]
    rot_true = resolved[:9]
    offsets = []
    for column in range(3):
        true_part = (
            rot_true[column] * resolved[9]
            + rot_true[3 + column] * resolved[10]
            + rot_true[6 + column] * resolved[11]
        )
        pred_part = (
            rot_pred[column] * pred_frames[9]
            + rot_pred[3 + column] * pred_frames[10]
            + rot_pred[6 + column] * pred_frames[11]
        )
        offsets.append(true_part - pred_part)
    return (rot_pred, rot_true, jnp.stack(offsets, axis=0), exists.reshape(residues * 8))


def atom_terms(true_atoms, atom_mask, residue_types, swap_flags):
    tables = residue_tables()
    onehot_int = type_onehot(residue_types).astype(jnp.int32)
    onehot = onehot_int.astype(jnp.float32)
    partner_table = jnp.asarray(tables[2], dtype=jnp.int32)
    atom_table = jnp.asarray(tables[0], dtype=jnp.float32)
    partners = jnp.sum(onehot_int[:, :, None] * partner_table[None], axis=1)
    own_slots = jnp.broadcast_to(jnp.arange(14, dtype=jnp.int32)[None, :], partners.shape)
    source = jnp.where(swap_flags[:, None] == 1, partners, own_slots)
    residues = residue_types.shape[0]
    shaped = true_atoms.reshape(3, residues, 14)
    resolved = jnp.take_along_axis(
        shaped, jnp.broadcast_to(source[None], shaped.shape), axis=2
    ).reshape(3, residues * 14)
    mask_resolved = jnp.take_along_axis(atom_mask.reshape(residues, 14), source, axis=1)
    exists = jnp.sum(onehot[:, :, None] * atom_table[None], axis=1)
    weight = (exists * mask_resolved.astype(jnp.float32)).reshape(residues * 14)
    return (resolved, weight)


def clamped_errors(frame_side, atom_side):
    rot_pred, rot_true, offset = frame_side
    pred_pos, true_pos = atom_side
    squares = jnp.zeros((offset.shape[1], pred_pos.shape[1]), jnp.float32)
    for column in range(3):
        error = offset[column][:, None]
        for axis_row in range(3):
            error = error + rot_pred[3 * axis_row + column][:, None] * pred_pos[axis_row][None, :]
            error = error - rot_true[3 * axis_row + column][:, None] * true_pos[axis_row][None, :]
        squares = squares + error * error
    return jnp.minimum(jnp.sqrt(squares + eps_square), clamp_length) / clamp_length


def block_groups(shard_count, shard_cols, pair_limit):
    groups = max(1, min(shard_count, pair_limit // shard_cols))
    while shard_count % groups:
        groups -= 1
    lane_step = 128 // math.gcd(shard_cols, 128)
    return groups


def pair_folder(frame_side, row_exists, shard_cols):
    frame_rows = row_exists.shape[0]
    pair_limit = max(shard_cols, (1 << 20) // frame_rows)

    def add_pairs(carry, pieces, start):
        length = pieces[0].shape[1]
        block_width = length
        shard_count = length // shard_cols
        block_width = block_groups(shard_count, shard_cols, pair_limit) * shard_cols
        turn_count = length // block_width

        def one_block(turn_index, running):
            frame_raw, atom_sum = running
            begin_at = turn_index * block_width
            pred_block = lax.dynamic_slice_in_dim(pieces[0], begin_at, block_width, 1)
            true_block = lax.dynamic_slice_in_dim(pieces[1], begin_at, block_width, 1)
            weight_block = lax.dynamic_slice_in_dim(pieces[2], begin_at, block_width, 1)
            clamped = clamped_errors(frame_side, (pred_block, true_block))
            frame_raw = frame_raw + jnp.sum(clamped * weight_block, axis=1)
            column_sums = jnp.sum(clamped * row_exists[:, None], axis=0)
            atom_sum = lax.dynamic_update_slice_in_dim(atom_sum, column_sums, begin_at, 0)
            return (frame_raw, atom_sum)

        return lax.fori_loop(0, turn_count, one_block, carry)

    return add_pairs


def shards(pred_frames, true_frames, pred_atoms, true_atoms, atom_mask, residue_types, swap_flags):
    rot_pred, rot_true, offset, exists = frame_terms(
        pred_frames, true_frames, residue_types, swap_flags
    )
    true_resolved, weight = atom_terms(true_atoms, atom_mask, residue_types, swap_flags)
    shard_cols = pred_atoms.shape[1]
    rows = side_by_side((rot_pred, rot_true, offset, exists[None, :]), GY, 1, 0)
    row_exists = rows[3][0]
    folder = pair_folder((rows[0], rows[1], rows[2]), row_exists, shard_cols)
    start_state = (
        jnp.zeros(row_exists.shape, jnp.float32),
        jnp.zeros((shard_cols * lax.axis_size(GX),), jnp.float32),
    )
    row_raw, column_sum = folder(
        start_state,
        gather_turned((pred_atoms, true_resolved, weight[None, :]), GX, (1, 1, 1)),
        jnp.int32(0),
    )
    frame_raw = sent_and_summed(row_raw, GY, 0)
    atom_part = sent_and_summed(column_sum, GX, 0)
    frame_sum = exists * frame_raw
    loss_sum, frame_count, atom_count = (
        by_axis(jnp.sum(frame_sum), GX_GY),
        by_axis(jnp.sum(exists), GX_GY),
        by_axis(jnp.sum(weight), GX_GY),
    )
    frame_loss = frame_sum / atom_count
    atom_loss = weight * atom_part / frame_count
    total_loss = (loss_sum / (frame_count * atom_count)).reshape(1)
    return (frame_loss, atom_loss, total_loss)


def solution(mesh):
    finer = Mesh(
        mesh.devices.reshape(mesh.shape["sa"], 8, 2, 4, 2), ("sa", "gx_0", "gx_1", "gy_0", "gy_1")
    )
    placed = (
        P(None, SA_GX_GY),
        P(None, SA_GX_GY),
        P(None, SA_GX_GY),
        P(None, SA_GX_GY),
        P(SA_GX_GY),
        P(SA_GX_GY),
        P(SA_GX_GY),
    )
    return jax.shard_map(
        shards,
        mesh=finer,
        in_specs=placed,
        out_specs=(P(SA_GX_GY), P(SA_GX_GY), P("sa")),
        check_vma=False,
    )
```

profile of v0, /device:TPU:2, one launch (start us, length us, event | category | flops | bytes accessed | tf_op | source)
XLA Modules:
  0.0 205.6 jit_solution(11149782708440451952)
XLA Ops:
  5.9 33.8 %all_gather.6 = f32[22,1024]{1,0:T(8,128)S(1)} all-gather(f32[22,128]{1,0:T(8,128)S(1)} %concatenate.6), channel_id=1, replica_groups=mesh['sa'=2,'gx_0'=8,'gx_1'=2,'gy_0'=4,'gy_1'=2] {'gy_0','gy_1'}, dimensions={1}, use_global_device_ids=true | all-gather | bytes 101376 | tf_op jit(solution)/shard_map/all_gather | solution.py:21
  41.7 9.4 %gather_fusion = f32[672]{0:T(1024)S(1)} fusion(f32[3,16,14]{2,1,0:T(8,128)S(1)} %reshape.529, s32[672]{0:T(1024)S(1)} %reshape.532), kind=kCustom, calls=%fused_computation | custom fusion | bytes 13440 | tf_op jit(solution)/shard_map/jit(take_along_axis)/gather | solution.py:127
  51.2 1.9 gather_fusion.1
  53.2 18.7 %all-gather = f32[16,224,7]{1,2,0:T(8,128)S(1)} all-gather(f32[1,224,7]{1,2,0:T(8,128)S(1)} %maximum_bitcast_fusion), channel_id=1, replica_groups=mesh['sa'=2,'gx_0'=8,'gx_1'=2,'gy_0'=4,'gy_1'=2] {'gx_0','gx_1'}, dimensions={0}, use_global_device_ids=true | all-gather | bytes 106624 | tf_op jit(solution)/shard_map/all_gather | solution.py:28
  72.1 70.5 %while.16 = (s32[]{:T(128)}, f32[1024]{0:T(1024)}, f32[3584]{0:T(1024)S(1)}, f32[3,1024]{1,0:T(4,128)S(1)}, f32[9,1024]{1,0:T(8,128)S(1)}, /*index=5*/f32[3,3584...) while((s32[]{:T(128)}, f32[1024]{0:T(1024)}, ...), condition=%wide.region_7.8_spmd.clone, body=%wide.region_4.7_spmd.clone.sunk | while | flops 82577416 | bytes 480513 | solution.py:180
  72.4 8.3 %multiply_reduce_fusion.15 = f32[896]{0:T(1024)S(1)} fusion(f32[1024]{0:T(1024)S(1)} %bitcast.147, f32[1024]{0:T(1024)S(1)} %bitcast.125, f32[1024]{0:T(1024)S(1)} %bitcast.107, f32[1024]{0:T(1024)S(1)} %bitcast.127, f32[1024]{0:T(1024)S(1)} %bitcast.109, f32[1024]{0:T(1024)S(1)} %bitcast.129, f32[1024]{0:T(1024)S(1)} %bitcast.111, ...), kind=kLoop, calls=%fused_computation.2.clone.1 | loop fusion | flops 41286784 | bytes 115200 | tf_op jit(solution)/shard_map/while/body/eval_jaxpr/reduce_sum | solution.py:176
  80.7 7.8 %multiply_reduce_fusion.14 = f32[1024]{0:T(1024)S(1)} fusion(f32[896]{0:T(1024)S(1)} %multiply_reduce_fusion.13, f32[1024]{0:T(1024)S(1)} %bitcast.126, f32[1024]{0:T(1024)S(1)} %bitcast.108, f32[1024]{0:T(1024)S(1)} %bitcast.128, f32[1024]{0:T(1024)S(1)} %bitcast.110, f32[1024]{0:T(1024)S(1)} %bitcast.130, f32[1024]{0:T(1024)S(1)} %bitcast.112, ...), kind=kLoop, calls=%fused_computation.3.clone.1 | loop fusion | flops 41286656 | bytes 115200 | tf_op jit(solution)/shard_map/while/body/eval_jaxpr/reduce_sum | solution.py:175
  89.5 8.3 %multiply_reduce_fusion.15 = f32[896]{0:T(1024)S(1)} fusion(f32[1024]{0:T(1024)S(1)} %bitcast.147, f32[1024]{0:T(1024)S(1)} %bitcast.125, f32[1024]{0:T(1024)S(1)} %bitcast.107, f32[1024]{0:T(1024)S(1)} %bitcast.127, f32[1024]{0:T(1024)S(1)} %bitcast.109, f32[1024]{0:T(1024)S(1)} %bitcast.129, f32[1024]{0:T(1024)S(1)} %bitcast.111, ...), kind=kLoop, calls=%fused_computation.2.clone.1 | loop fusion | flops 41286784 | bytes 115200 | tf_op jit(solution)/shard_map/while/body/eval_jaxpr/reduce_sum | solution.py:176
  97.8 7.8 %multiply_reduce_fusion.14 = f32[1024]{0:T(1024)S(1)} fusion(f32[896]{0:T(1024)S(1)} %multiply_reduce_fusion.13, f32[1024]{0:T(1024)S(1)} %bitcast.126, f32[1024]{0:T(1024)S(1)} %bitcast.108, f32[1024]{0:T(1024)S(1)} %bitcast.128, f32[1024]{0:T(1024)S(1)} %bitcast.110, f32[1024]{0:T(1024)S(1)} %bitcast.130, f32[1024]{0:T(1024)S(1)} %bitcast.112, ...), kind=kLoop, calls=%fused_computation.3.clone.1 | loop fusion | flops 41286656 | bytes 115200 | tf_op jit(solution)/shard_map/while/body/eval_jaxpr/reduce_sum | solution.py:175
  105.6 1.3 select_add_fusion.2
  107.3 8.3 %multiply_reduce_fusion.15 = f32[896]{0:T(1024)S(1)} fusion(f32[1024]{0:T(1024)S(1)} %bitcast.147, f32[1024]{0:T(1024)S(1)} %bitcast.125, f32[1024]{0:T(1024)S(1)} %bitcast.107, f32[1024]{0:T(1024)S(1)} %bitcast.127, f32[1024]{0:T(1024)S(1)} %bitcast.109, f32[1024]{0:T(1024)S(1)} %bitcast.129, f32[1024]{0:T(1024)S(1)} %bitcast.111, ...), kind=kLoop, calls=%fused_computation.2.clone.1 | loop fusion | flops 41286784 | bytes 115200 | tf_op jit(solution)/shard_map/while/body/eval_jaxpr/reduce_sum | solution.py:176
  115.5 7.8 %multiply_reduce_fusion.14 = f32[1024]{0:T(1024)S(1)} fusion(f32[896]{0:T(1024)S(1)} %multiply_reduce_fusion.13, f32[1024]{0:T(1024)S(1)} %bitcast.126, f32[1024]{0:T(1024)S(1)} %bitcast.108, f32[1024]{0:T(1024)S(1)} %bitcast.128, f32[1024]{0:T(1024)S(1)} %bitcast.110, f32[1024]{0:T(1024)S(1)} %bitcast.130, f32[1024]{0:T(1024)S(1)} %bitcast.112, ...), kind=kLoop, calls=%fused_computation.3.clone.1 | loop fusion | flops 41286656 | bytes 115200 | tf_op jit(solution)/shard_map/while/body/eval_jaxpr/reduce_sum | solution.py:175
  123.4 1.3 select_add_fusion.2
  125.1 8.3 %multiply_reduce_fusion.15 = f32[896]{0:T(1024)S(1)} fusion(f32[1024]{0:T(1024)S(1)} %bitcast.147, f32[1024]{0:T(1024)S(1)} %bitcast.125, f32[1024]{0:T(1024)S(1)} %bitcast.107, f32[1024]{0:T(1024)S(1)} %bitcast.127, f32[1024]{0:T(1024)S(1)} %bitcast.109, f32[1024]{0:T(1024)S(1)} %bitcast.129, f32[1024]{0:T(1024)S(1)} %bitcast.111, ...), kind=kLoop, calls=%fused_computation.2.clone.1 | loop fusion | flops 41286784 | bytes 115200 | tf_op jit(solution)/shard_map/while/body/eval_jaxpr/reduce_sum | solution.py:176
  133.3 7.8 %multiply_reduce_fusion.14 = f32[1024]{0:T(1024)S(1)} fusion(f32[896]{0:T(1024)S(1)} %multiply_reduce_fusion.13, f32[1024]{0:T(1024)S(1)} %bitcast.126, f32[1024]{0:T(1024)S(1)} %bitcast.108, f32[1024]{0:T(1024)S(1)} %bitcast.128, f32[1024]{0:T(1024)S(1)} %bitcast.110, f32[1024]{0:T(1024)S(1)} %bitcast.130, f32[1024]{0:T(1024)S(1)} %bitcast.112, ...), kind=kLoop, calls=%fused_computation.3.clone.1 | loop fusion | flops 41286656 | bytes 115200 | tf_op jit(solution)/shard_map/while/body/eval_jaxpr/reduce_sum | solution.py:175
  141.2 1.3 select_add_fusion.2
  142.6 9.2 %all-to-all-start = ((f32[8,1,128]{2,1,0:T(1,128)}), f32[8,1,128]{2,1,0:T(1,128)S(1)}, u32[]{:S(2)}, u32[]{:S(2)}) async-start(f32[8,1,128]{2,1,0:T(1,128)} %bitcast.8), calls=%async_computation | async-start | bytes 8192 | tf_op jit(solution)/shard_map/all_to_all | solution.py:44
  153.7 4.2 %all-to-all-done = f32[8,1,128]{2,1,0:T(1,128)S(1)} async-done(((f32[8,1,128]{2,1,0:T(1,128)}), f32[8,1,128]{2,1,0:T(1,128)S(1)}, u32[]{:S(2)}, u32[]{:S(2)}) %all-to-all-start) | async-done | bytes 4128 | tf_op jit(solution)/shard_map/all_to_all | solution.py:44
  157.9 3.7 %all-to-all-start.1 = ((f32[16,1,224]{2,1,0:T(1,128)}), f32[16,1,224]{2,1,0:T(1,128)S(1)}, u32[]{:S(2)}, u32[]{:S(2)}) async-start(f32[16,1,224]{2,1,0:T(1,128)} %all_to_all.14), calls=%async_computation.1 | async-start | bytes 32768 | tf_op jit(solution)/shard_map/all_to_all | solution.py:44
  162.3 17.9 %all-reduce = (f32[]{:T(128)}, f32[]{:T(128)}, f32[]{:T(128)}) all-reduce(f32[]{:T(128)} %multiply_reduce_fusion.8, f32[]{:T(128)} %get-tuple-element.214, f32[]{:T(128)} %multiply_reduce_fusion.9), channel_id=1, replica_groups=mesh['sa'=2,'gx_0'=8,'gx_1'=2,'gy_0'=4,'gy_1'=2] {'gx_0'}, use_global_device_ids=true, to_apply=%region_10.11 | all-reduce | flops 3 | bytes 24 | tf_op jit(solution)/shard_map/psum | solution.py:49
  180.2 3.1 %all-reduce.3 = (f32[]{:T(128)}, f32[]{:T(128)}, f32[]{:T(128)}) all-reduce(f32[]{:T(128)} %get-tuple-element.237, f32[]{:T(128)} %get-tuple-element.238, f32[]{:T(128)} %get-tuple-element.239), channel_id=1, replica_groups=mesh['sa'=2,'gx_0'=8,'gx_1'=2,'gy_0'=4,'gy_1'=2] {'gx_1'}, use_global_device_ids=true, to_apply=%region_11.12 | all-reduce | flops 3 | bytes 24 | tf_op jit(solution)/shard_map/psum | solution.py:49
  183.3 10.0 %all-reduce.1 = (f32[]{:T(128)}, f32[]{:T(128)}, f32[]{:T(128)}) all-reduce(f32[]{:T(128)} %get-tuple-element.246, f32[]{:T(128)} %get-tuple-element.247, f32[]{:T(128)} %get-tuple-element.248), channel_id=1, replica_groups=mesh['sa'=2,'gx_0'=8,'gx_1'=2,'gy_0'=4,'gy_1'=2] {'gy_0'}, use_global_device_ids=true, to_apply=%region_12.13 | all-reduce | flops 3 | bytes 24 | tf_op jit(solution)/shard_map/psum | solution.py:49
  193.2 7.1 %all-reduce.2 = (f32[]{:T(128)}, f32[]{:T(128)}, f32[]{:T(128)}) all-reduce(f32[]{:T(128)} %get-tuple-element.240, f32[]{:T(128)} %get-tuple-element.241, f32[]{:T(128)} %get-tuple-element.242), channel_id=1, replica_groups=mesh['sa'=2,'gx_0'=8,'gx_1'=2,'gy_0'=4,'gy_1'=2] {'gy_1'}, use_global_device_ids=true, to_apply=%region_13.14 | all-reduce | flops 3 | bytes 24 | tf_op jit(solution)/shard_map/psum | solution.py:49
  200.3 1.2 broadcast_divide_fusion
  (114 shorter events, 13.1 us)
Async XLA Ops:
  0.6 3.5 %copy-start.2 = (f32[12,128]{1,0:T(8,128)S(1)}, f32[12,128]{1,0:T(8,128)}, u32[]{:S(2)}) copy-start(f32[12,128]{1,0:T(8,128)} %param.15) | copy-start | bytes 18436
  2.0 2.3 %copy-start.5 = (f32[20,8]{0,1:T(8,128)S(1)}, f32[20,8]{0,1:T(8,128)}, u32[]{:S(2)}) copy-start(f32[20,8]{0,1:T(8,128)} %constant.99.clone) | copy-start | bytes 1924
  2.0 2.3 %copy-start.6 = (f32[20,8]{0,1:T(8,128)S(1)}, f32[20,8]{0,1:T(8,128)}, u32[]{:S(2)}) copy-start(f32[20,8]{0,1:T(8,128)} %constant.98.clone) | copy-start | bytes 1924
  3.7 1.2 copy-start.8
  5.1 0.7 copy-start
  39.7 0.7 copy-start.7
  39.7 1.1 copy-start.3
  39.8 1.2 copy-start.1
  51.2 2.0 copy-start.4
  142.6 15.3 %all-to-all-start = ((f32[8,1,128]{2,1,0:T(1,128)}), f32[8,1,128]{2,1,0:T(1,128)S(1)}, u32[]{:S(2)}, u32[]{:S(2)}) async-start(f32[8,1,128]{2,1,0:T(1,128)} %bitcast.8), calls=%async_computation | async-start | bytes 8192 | tf_op jit(solution)/shard_map/all_to_all | solution.py:44
  157.9 45.4 %all-to-all-start.1 = ((f32[16,1,224]{2,1,0:T(1,128)}), f32[16,1,224]{2,1,0:T(1,128)S(1)}, u32[]{:S(2)}, u32[]{:S(2)}) async-start(f32[16,1,224]{2,1,0:T(1,128)} %all_to_all.14), calls=%async_computation.1 | async-start | bytes 32768 | tf_op jit(solution)/shard_map/all_to_all | solution.py:44
where the time goes:
time: 206 us
  blocking collectives  90.5 us (44%)
  other arithmetic  76.6 us (37%)
  local copies, waits for them, and re-layouts  17.1 us (8%)
  starting transfers between devices  13 us (6%)
  waiting for transfers between devices  4.23 us (2%)
  between operations  4.01 us (2%)
    psum x4, blocking collectives, by_axis(): return functools.reduce(lax.psum, axes, value)  38 us
    all_gather x1, blocking collectives, side_by_side(): result = lax.all_gather(both, axis, axis=dim, tiled=True)  33.8 us
    reduce_sum x4, other arithmetic, one_block(): column_sums = jnp.sum(clamped * row_exists[:, None], axis=0)  33 us
    reduce_sum x4, other arithmetic, one_block(): frame_raw = frame_raw + jnp.sum(clamped * weight_block, axis=1)  31.3 us
    all_gather x1, blocking collectives, gather_turned(): lax.all_gather(both, axis, axis=0, tiled=True)  18.7 us
    all_to_all x2, starting transfers between devices, sent_and_summed(): lax.all_to_all(tiles, axis, split_axis=0, concat_axis=0, tiled=True)  13 us
    gather x3, local copies, waits for them, and re-layouts, atom_terms(): jnp.take_along_axis(shaped, jnp.broadcast_to(source[None], shaped.shape),...  9.56 us
    add x4, other arithmetic, one_block(): frame_raw = frame_raw + jnp.sum(clamped * weight_block, axis=1)  4.41 us
  transfers between devices with their start and end apart: 2, of which 1 were waited for; matrix products, arithmetic and copies ran while one was open for 1% of the time, Pallas kernels for 0%

commit v1 on v0

--- a/solution.py
+++ b/solution.py
@@ -25,7 +25,13 @@
 def gather_turned(arrays, axis, dims):
     turned = [jnp.moveaxis(a, dim, 0) for a, dim in zip(arrays, dims)]
     both = jnp.concatenate([t.reshape(len(t), -1) for t in turned], axis=1)
-    result, at, gathered = (lax.all_gather(both, axis, axis=0, tiled=True), 0, [])
+    result, at, gathered = (
+        jnp.concatenate(
+            lax.all_to_all(jnp.stack([both] * lax.axis_size(axis), axis=0), axis, 0, 0), axis=0
+        ),
+        0,
+        [],
+    )
     for t, dim in zip(turned, dims):
         piece = result[:, at : at + t[0].size].reshape(-1, *t.shape[1:])
         gathered.append(jnp.moveaxis(piece, 0, dim))

time: 206 us -> 198 us (0.961)
  blocking collectives: 90.5 us -> 70.2 us
  starting transfers between devices: 13 us -> 25.2 us
    all_gather x1 -> x0, blocking collectives: 18.7 us -> none  [gather_turned(): lax.all_gather(both, axis, axis=0, tiled=True)]
    all_to_all x0 -> x1, starting transfers between devices: none -> 8.71 us  [gather_turned(): lax.all_to_all(jnp.stack([both] * lax.axis_size(axis), axis=0), axis, 0, 0)]
    all_to_all x2, starting transfers between devices: 13 us -> 16.5 us  [sent_and_summed(): lax.all_to_all(tiles, axis, split_axis=0, concat_axis=0, tiled=True)]
  transfers between devices with their start and end apart: 2 -> 3, of which waited for: 1 -> 1; matrix products, arithmetic and copies ran while one was open for 1% -> 2% of each run, Pallas kernels for 0% -> 0%
where the time goes in v1:
time: 198 us; the launch traced here: 197 us
  other arithmetic  75.7 us (38%)
  blocking collectives  70.2 us (35%)
  starting transfers between devices  25.2 us (13%)
  local copies, waits for them, and re-layouts  17.5 us (9%)
  waiting for transfers between devices  4.41 us (2%)
  between operations  4.06 us (2%)
    psum x4, blocking collectives, by_axis(): return functools.reduce(lax.psum, axes, value)  38 us
    reduce_sum x4, other arithmetic, one_block(): column_sums = jnp.sum(clamped * row_exists[:, None], axis=0)  32.8 us
    all_gather x1, blocking collectives, side_by_side(): result = lax.all_gather(both, axis, axis=dim, tiled=True)  32.2 us
    reduce_sum x4, other arithmetic, one_block(): frame_raw = frame_raw + jnp.sum(clamped * weight_block, axis=1)  31.3 us
    all_to_all x2, starting transfers between devices, sent_and_summed(): lax.all_to_all(tiles, axis, split_axis=0, concat_axis=0, tiled=True)  16.5 us
    gather x3, local copies, waits for them, and re-layouts, atom_terms(): jnp.take_along_axis(shaped, jnp.broadcast_to(source[None], shaped.shape),...  9.56 us
    all_to_all x1, starting transfers between devices, gather_turned(): lax.all_to_all(jnp.stack([both] * lax.axis_size(axis), axis=0), axis, 0, 0)  8.71 us
    all_to_all x2, waiting for transfers between devices, sent_and_summed(): lax.all_to_all(tiles, axis, split_axis=0, concat_axis=0, tiled=True)  4.41 us
  transfers between devices with their start and end apart: 3, of which 1 were waited for; matrix products, arithmetic and copies ran while one was open for 2% of the time, Pallas kernels for 0%

profile of v1, /device:TPU:2, one launch (start us, length us, event | category | flops | bytes accessed | tf_op | source)
XLA Modules:
  0.0 197.1 jit_solution(9959082825866582214)
XLA Ops:
  5.1 9.4 %gather_fusion = f32[672]{0:T(1024)S(1)} fusion(f32[3,16,14]{2,1,0:T(8,128)S(1)} %reshape.534, s32[672]{0:T(1024)S(1)} %reshape.538), kind=kCustom, calls=%fused_computation | custom fusion | bytes 13440 | tf_op jit(solution)/shard_map/jit(take_along_axis)/gather | solution.py:133
  14.6 1.9 gather_fusion.1
  17.3 8.7 %all-to-all-start = ((f32[16,224,7]{1,2,0:T(8,128)}), f32[16,224,7]{1,2,0:T(8,128)S(1)}, u32[]{:S(2)}, u32[]{:S(2)}) async-start(f32[16,224,7]{1,2,0:T(8,128)} %stack.2), calls=%async_computation | async-start | bytes 262144 | tf_op jit(solution)/shard_map/all_to_all | solution.py:30
  27.9 32.2 %all_gather.3 = f32[22,1024]{1,0:T(8,128)S(1)} all-gather(f32[22,128]{1,0:T(8,128)S(1)} %concatenate.6), channel_id=1, replica_groups=mesh['sa'=2,'gx_0'=8,'gx_1'=2,'gy_0'=4,'gy_1'=2] {'gy_0','gy_1'}, dimensions={1}, use_global_device_ids=true | all-gather | bytes 101376 | tf_op jit(solution)/shard_map/all_gather | solution.py:21
  60.4 70.2 %while.16 = (s32[]{:T(128)}, f32[1024]{0:T(1024)}, f32[3584]{0:T(1024)S(1)}, f32[3,1024]{1,0:T(4,128)S(1)}, f32[9,1024]{1,0:T(8,128)S(1)}, /*index=5*/f32[3,3584...) while((s32[]{:T(128)}, f32[1024]{0:T(1024)}, ...), condition=%wide.region_7.8_spmd.clone, body=%wide.region_4.7_spmd.clone.sunk | while | flops 82577416 | bytes 480513 | solution.py:186
  60.7 8.2 %multiply_reduce_fusion.15 = f32[896]{0:T(1024)S(1)} fusion(f32[1024]{0:T(1024)S(1)} %bitcast.145, f32[1024]{0:T(1024)S(1)} %bitcast.123, f32[1024]{0:T(1024)S(1)} %bitcast.105, f32[1024]{0:T(1024)S(1)} %bitcast.125, f32[1024]{0:T(1024)S(1)} %bitcast.107, f32[1024]{0:T(1024)S(1)} %bitcast.127, f32[1024]{0:T(1024)S(1)} %bitcast.109, ...), kind=kLoop, calls=%fused_computation.2.clone.1 | loop fusion | flops 41286784 | bytes 115200 | tf_op jit(solution)/shard_map/while/body/eval_jaxpr/reduce_sum | solution.py:182
  68.9 7.8 %multiply_reduce_fusion.14 = f32[1024]{0:T(1024)S(1)} fusion(f32[896]{0:T(1024)S(1)} %multiply_reduce_fusion.13, f32[1024]{0:T(1024)S(1)} %bitcast.124, f32[1024]{0:T(1024)S(1)} %bitcast.106, f32[1024]{0:T(1024)S(1)} %bitcast.126, f32[1024]{0:T(1024)S(1)} %bitcast.108, f32[1024]{0:T(1024)S(1)} %bitcast.128, f32[1024]{0:T(1024)S(1)} %bitcast.110, ...), kind=kLoop, calls=%fused_computation.3.clone.1 | loop fusion | flops 41286656 | bytes 115200 | tf_op jit(solution)/shard_map/while/body/eval_jaxpr/reduce_sum | solution.py:181
  77.7 8.2 %multiply_reduce_fusion.15 = f32[896]{0:T(1024)S(1)} fusion(f32[1024]{0:T(1024)S(1)} %bitcast.145, f32[1024]{0:T(1024)S(1)} %bitcast.123, f32[1024]{0:T(1024)S(1)} %bitcast.105, f32[1024]{0:T(1024)S(1)} %bitcast.125, f32[1024]{0:T(1024)S(1)} %bitcast.107, f32[1024]{0:T(1024)S(1)} %bitcast.127, f32[1024]{0:T(1024)S(1)} %bitcast.109, ...), kind=kLoop, calls=%fused_computation.2.clone.1 | loop fusion | flops 41286784 | bytes 115200 | tf_op jit(solution)/shard_map/while/body/eval_jaxpr/reduce_sum | solution.py:182
  85.9 7.8 %multiply_reduce_fusion.14 = f32[1024]{0:T(1024)S(1)} fusion(f32[896]{0:T(1024)S(1)} %multiply_reduce_fusion.13, f32[1024]{0:T(1024)S(1)} %bitcast.124, f32[1024]{0:T(1024)S(1)} %bitcast.106, f32[1024]{0:T(1024)S(1)} %bitcast.126, f32[1024]{0:T(1024)S(1)} %bitcast.108, f32[1024]{0:T(1024)S(1)} %bitcast.128, f32[1024]{0:T(1024)S(1)} %bitcast.110, ...), kind=kLoop, calls=%fused_computation.3.clone.1 | loop fusion | flops 41286656 | bytes 115200 | tf_op jit(solution)/shard_map/while/body/eval_jaxpr/reduce_sum | solution.py:181
  93.8 1.3 select_add_fusion.2
  95.5 8.2 %multiply_reduce_fusion.15 = f32[896]{0:T(1024)S(1)} fusion(f32[1024]{0:T(1024)S(1)} %bitcast.145, f32[1024]{0:T(1024)S(1)} %bitcast.123, f32[1024]{0:T(1024)S(1)} %bitcast.105, f32[1024]{0:T(1024)S(1)} %bitcast.125, f32[1024]{0:T(1024)S(1)} %bitcast.107, f32[1024]{0:T(1024)S(1)} %bitcast.127, f32[1024]{0:T(1024)S(1)} %bitcast.109, ...), kind=kLoop, calls=%fused_computation.2.clone.1 | loop fusion | flops 41286784 | bytes 115200 | tf_op jit(solution)/shard_map/while/body/eval_jaxpr/reduce_sum | solution.py:182
  103.7 7.8 %multiply_reduce_fusion.14 = f32[1024]{0:T(1024)S(1)} fusion(f32[896]{0:T(1024)S(1)} %multiply_reduce_fusion.13, f32[1024]{0:T(1024)S(1)} %bitcast.124, f32[1024]{0:T(1024)S(1)} %bitcast.106, f32[1024]{0:T(1024)S(1)} %bitcast.126, f32[1024]{0:T(1024)S(1)} %bitcast.108, f32[1024]{0:T(1024)S(1)} %bitcast.128, f32[1024]{0:T(1024)S(1)} %bitcast.110, ...), kind=kLoop, calls=%fused_computation.3.clone.1 | loop fusion | flops 41286656 | bytes 115200 | tf_op jit(solution)/shard_map/while/body/eval_jaxpr/reduce_sum | solution.py:181
  111.5 1.3 select_add_fusion.2
  113.2 8.2 %multiply_reduce_fusion.15 = f32[896]{0:T(1024)S(1)} fusion(f32[1024]{0:T(1024)S(1)} %bitcast.145, f32[1024]{0:T(1024)S(1)} %bitcast.123, f32[1024]{0:T(1024)S(1)} %bitcast.105, f32[1024]{0:T(1024)S(1)} %bitcast.125, f32[1024]{0:T(1024)S(1)} %bitcast.107, f32[1024]{0:T(1024)S(1)} %bitcast.127, f32[1024]{0:T(1024)S(1)} %bitcast.109, ...), kind=kLoop, calls=%fused_computation.2.clone.1 | loop fusion | flops 41286784 | bytes 115200 | tf_op jit(solution)/shard_map/while/body/eval_jaxpr/reduce_sum | solution.py:182
  121.4 7.8 %multiply_reduce_fusion.14 = f32[1024]{0:T(1024)S(1)} fusion(f32[896]{0:T(1024)S(1)} %multiply_reduce_fusion.13, f32[1024]{0:T(1024)S(1)} %bitcast.124, f32[1024]{0:T(1024)S(1)} %bitcast.106, f32[1024]{0:T(1024)S(1)} %bitcast.126, f32[1024]{0:T(1024)S(1)} %bitcast.108, f32[1024]{0:T(1024)S(1)} %bitcast.128, f32[1024]{0:T(1024)S(1)} %bitcast.110, ...), kind=kLoop, calls=%fused_computation.3.clone.1 | loop fusion | flops 41286656 | bytes 115200 | tf_op jit(solution)/shard_map/while/body/eval_jaxpr/reduce_sum | solution.py:181
  129.2 1.3 select_add_fusion.2
  130.6 9.2 %all-to-all-start.1 = ((f32[8,1,128]{2,1,0:T(1,128)}), f32[8,1,128]{2,1,0:T(1,128)S(1)}, u32[]{:S(2)}, u32[]{:S(2)}) async-start(f32[8,1,128]{2,1,0:T(1,128)} %bitcast.7), calls=%async_computation.1 | async-start | bytes 8192 | tf_op jit(solution)/shard_map/all_to_all | solution.py:50
  141.5 4.4 %all-to-all-done.1 = f32[8,1,128]{2,1,0:T(1,128)S(1)} async-done(((f32[8,1,128]{2,1,0:T(1,128)}), f32[8,1,128]{2,1,0:T(1,128)S(1)}, u32[]{:S(2)}, u32[]{:S(2)}) %all-to-all-start.1) | async-done | bytes 4128 | tf_op jit(solution)/shard_map/all_to_all | solution.py:50
  145.9 7.2 %all-to-all-start.2 = ((f32[16,1,224]{2,1,0:T(1,128)}), f32[16,1,224]{2,1,0:T(1,128)S(1)}, u32[]{:S(2)}, u32[]{:S(2)}) async-start(f32[16,1,224]{2,1,0:T(1,128)} %all_to_all.18), calls=%async_computation.2 | async-start | bytes 32768 | tf_op jit(solution)/shard_map/all_to_all | solution.py:50
  153.8 17.9 %all-reduce = (f32[]{:T(128)}, f32[]{:T(128)}, f32[]{:T(128)}) all-reduce(f32[]{:T(128)} %multiply_reduce_fusion.8, f32[]{:T(128)} %get-tuple-element.214, f32[]{:T(128)} %multiply_reduce_fusion.9), channel_id=1, replica_groups=mesh['sa'=2,'gx_0'=8,'gx_1'=2,'gy_0'=4,'gy_1'=2] {'gx_0'}, use_global_device_ids=true, to_apply=%region_10.11 | all-reduce | flops 3 | bytes 24 | tf_op jit(solution)/shard_map/psum | solution.py:55
  171.7 3.1 %all-reduce.3 = (f32[]{:T(128)}, f32[]{:T(128)}, f32[]{:T(128)}) all-reduce(f32[]{:T(128)} %get-tuple-element.237, f32[]{:T(128)} %get-tuple-element.238, f32[]{:T(128)} %get-tuple-element.239), channel_id=1, replica_groups=mesh['sa'=2,'gx_0'=8,'gx_1'=2,'gy_0'=4,'gy_1'=2] {'gx_1'}, use_global_device_ids=true, to_apply=%region_11.12 | all-reduce | flops 3 | bytes 24 | tf_op jit(solution)/shard_map/psum | solution.py:55
  174.8 10.0 %all-reduce.1 = (f32[]{:T(128)}, f32[]{:T(128)}, f32[]{:T(128)}) all-reduce(f32[]{:T(128)} %get-tuple-element.246, f32[]{:T(128)} %get-tuple-element.247, f32[]{:T(128)} %get-tuple-element.248), channel_id=1, replica_groups=mesh['sa'=2,'gx_0'=8,'gx_1'=2,'gy_0'=4,'gy_1'=2] {'gy_0'}, use_global_device_ids=true, to_apply=%region_12.13 | all-reduce | flops 3 | bytes 24 | tf_op jit(solution)/shard_map/psum | solution.py:55
  184.7 7.1 %all-reduce.2 = (f32[]{:T(128)}, f32[]{:T(128)}, f32[]{:T(128)}) all-reduce(f32[]{:T(128)} %get-tuple-element.240, f32[]{:T(128)} %get-tuple-element.241, f32[]{:T(128)} %get-tuple-element.242), channel_id=1, replica_groups=mesh['sa'=2,'gx_0'=8,'gx_1'=2,'gy_0'=4,'gy_1'=2] {'gy_1'}, use_global_device_ids=true, to_apply=%region_13.14 | all-reduce | flops 3 | bytes 24 | tf_op jit(solution)/shard_map/psum | solution.py:55
  191.8 1.2 broadcast_divide_fusion
  (118 shorter events, 12.8 us)
Async XLA Ops:
  0.6 3.7 %copy-start.1 = (f32[20,14]{0,1:T(8,128)S(1)}, f32[20,14]{0,1:T(8,128)}, u32[]{:S(2)}) copy-start(f32[20,14]{0,1:T(8,128)} %constant.102.clone) | copy-start | bytes 3364
  0.6 3.2 %copy-start.7 = (s32[224]{0:T(256)S(1)}, s32[224]{0:T(256)}, u32[]{:S(2)}) copy-start(s32[224]{0:T(256)} %param.18) | copy-start | bytes 2692
  0.7 3.6 %copy-start.3 = (f32[3,224]{1,0:T(4,128)S(1)}, f32[3,224]{1,0:T(4,128)}, u32[]{:S(2)}) copy-start(f32[3,224]{1,0:T(4,128)} %param.17) | copy-start | bytes 8068
  14.6 2.0 %copy-start.4 = (f32[3,224]{1,0:T(4,128)S(1)}, f32[3,224]{1,0:T(4,128)}, u32[]{:S(2)}) copy-start(f32[3,224]{1,0:T(4,128)} %param.16) | copy-start | bytes 8068
  17.2 8.7 %copy-start.9 = (s32[16]{0:T(128)S(1)}, s32[16]{0:T(128)}, u32[]{:S(2)}) copy-start(s32[16]{0:T(128)} %param.20) | copy-start | bytes 196
  17.2 8.9 %copy-start.2 = (f32[12,128]{1,0:T(8,128)S(1)}, f32[12,128]{1,0:T(8,128)}, u32[]{:S(2)}) copy-start(f32[12,128]{1,0:T(8,128)} %param.15) | copy-start | bytes 18436
  17.3 9.0 %copy-start.5 = (f32[20,8]{0,1:T(8,128)S(1)}, f32[20,8]{0,1:T(8,128)}, u32[]{:S(2)}) copy-start(f32[20,8]{0,1:T(8,128)} %constant.99.clone) | copy-start | bytes 1924
  17.3 9.0 %copy-start.6 = (f32[20,8]{0,1:T(8,128)S(1)}, f32[20,8]{0,1:T(8,128)}, u32[]{:S(2)}) copy-start(f32[20,8]{0,1:T(8,128)} %constant.98.clone) | copy-start | bytes 1924
  17.3 42.9 %all-to-all-start = ((f32[16,224,7]{1,2,0:T(8,128)}), f32[16,224,7]{1,2,0:T(8,128)S(1)}, u32[]{:S(2)}, u32[]{:S(2)}) async-start(f32[16,224,7]{1,2,0:T(8,128)} %stack.2), calls=%async_computation | async-start | bytes 262144 | tf_op jit(solution)/shard_map/all_to_all | solution.py:30
  26.0 1.0 copy-start.8
  27.0 0.7 copy-start
  130.6 15.3 %all-to-all-start.1 = ((f32[8,1,128]{2,1,0:T(1,128)}), f32[8,1,128]{2,1,0:T(1,128)S(1)}, u32[]{:S(2)}, u32[]{:S(2)}) async-start(f32[8,1,128]{2,1,0:T(1,128)} %bitcast.7), calls=%async_computation.1 | async-start | bytes 8192 | tf_op jit(solution)/shard_map/all_to_all | solution.py:50
  145.9 48.9 %all-to-all-start.2 = ((f32[16,1,224]{2,1,0:T(1,128)}), f32[16,1,224]{2,1,0:T(1,128)S(1)}, u32[]{:S(2)}, u32[]{:S(2)}) async-start(f32[16,1,224]{2,1,0:T(1,128)} %all_to_all.18), calls=%async_computation.2 | async-start | bytes 32768 | tf_op jit(solution)/shard_map/all_to_all | solution.py:50
